TPU v7x, 32 devices: a whole 2x2x4 slice. The times are simulated.
32 devices in a mesh: groups: 2 (over y), tok: 16 (over z, x, core).
Axes of the slice: x: 2, y: 2, z: 4, core: 2. Of those that a mesh axis runs over, the one named last changes fastest.
Arguments:
- queries: bfloat16 [1024, 2048], P(('groups', 'tok')), parts along dimension 0, may hold values from -6 to 6
- new_kv: bfloat16 [3072, 4096], P(('groups', 'tok')), parts along dimension 0, may hold values from -6 to 6
- prev_kv: bfloat16 [2, 3072, 4096], P(None, ('groups', 'tok')), parts along dimension 1, may hold values from -6 to 6
- base_step: int32 [32], P(('groups', 'tok')), parts along dimension 0, may hold values from 0 to 1
- live_counts: int32 [32], P('groups'), parts along dimension 0, may hold values from 1 to 96
- sketch: float32 [4096, 32], replicated, may hold values from -0.09375 to 0.09375
- cache: bfloat16 [64, 1536, 128], P(('groups', 'tok')), parts along dimension 0, may hold values from -6 to 6, as said below
- w_out: bfloat16 [2048, 1536], replicated, may hold values from -0.125 to 0.125
Outputs:
- projected: bfloat16 [1024, 1536], P(('groups', 'tok')), parts along dimension 0
There are 2 independent parts, one for each index of `groups`. A program takes and returns all parts, laid end to end along the dimension named above; an argument that names none is the same for every part. Nothing has to cross between parts.
Inputs may be any that keep to these rules, and one draw needn't show every extreme that they name: cache slots i and j hold the same values when i // 2 == j // 2 and i % 2 == j % 2.
All inputs are finite; a program needn't handle non-finite values.
Results may differ from a plain program's by a relative error of at most 0.019.
Values may be sent and summed in bfloat16 or wider, within the bound.
No kernel may reach another device: no remote copies, remote signals or barrier semaphores. Data moves between devices by JAX's collectives and lax.ppermute only.
A program may use at most 128 MiB of HBM per device.

v0:
```python
import math
import jax
import jax.numpy as jnp
from jax import lax
from jax.sharding import PartitionSpec as P

HD = 64
SWEEPS = 2
highest = lax.Precision.HIGHEST


def orthonormal(block_cols):
    gram_matrix = jnp.dot(block_cols.T, block_cols, precision=highest)
    lower_factor = jnp.linalg.cholesky(gram_matrix)
    return jax.scipy.linalg.solve_triangular(lower_factor, block_cols.T, lower=True).T


def compress(delta_block, sketch):
    basis_cols = orthonormal(jnp.dot(delta_block, sketch, precision=highest))
    for sweep_index in range(SWEEPS):
        inner = jnp.dot(delta_block.T, basis_cols, precision=highest)
        basis_cols = orthonormal(jnp.dot(delta_block, inner, precision=highest))
    right_factor = jnp.dot(basis_cols.T, delta_block, precision=highest)
    return (basis_cols.astype(jnp.bfloat16), right_factor.astype(jnp.bfloat16))


def spread_heads(matrix, head_groups, groups_q, width):
    lead = matrix.shape[0]
    per_group = matrix.reshape(lead, head_groups, width).transpose(1, 0, 2)
    copies = jnp.broadcast_to(per_group[:, None], (head_groups, groups_q, lead, width))
    return copies.reshape(head_groups * groups_q, lead, width)


def attend_head(pieces, live_keys):
    q_head, keys_values = pieces
    key_part = keys_values[:, :HD]
    value_part = keys_values[:, HD:]
    query_count = q_head.shape[0]
    block_rows = math.gcd(query_count, 512)

    def one_block(query_block):
        scores = jnp.dot(query_block, key_part.T, preferred_element_type=jnp.float32) * HD ** (-0.5)
        scores = jnp.where(live_keys[None, :], scores, -1e30)
        row_max = jnp.max(scores, axis=-1, keepdims=True)
        exponent = jnp.exp(scores - row_max)
        weights = (exponent / jnp.sum(exponent, axis=-1, keepdims=True)).astype(jnp.bfloat16)
        return jnp.dot(weights, value_part, preferred_element_type=jnp.float32).astype(jnp.bfloat16)

    return lax.map(one_block, q_head.reshape(query_count // block_rows, block_rows, HD)).reshape(
        query_count, HD
    )


def per_device(queries, new_kv, prev_kv, base_step, live_counts, sketch, cache, w_out):
    shards = lax.axis_size("tok")
    tok_rows = new_kv.shape[0]
    query_rows = queries.shape[0]
    head_count = queries.shape[1] // HD
    groups_q = max(1, shards // head_count)
    per_dev = head_count * groups_q // shards
    head_groups = head_count // per_dev
    part_rows = query_rows // groups_q
    width = per_dev * 2 * HD
    key_count = shards * tok_rows
    query_count = shards * part_rows
    prior = prev_kv[0].astype(jnp.float32)
    prior = jnp.where(base_step[0] == 1, prev_kv[1].astype(jnp.float32), prior)
    delta = new_kv.astype(jnp.float32) - prior
    left_factor, right_factor = compress(delta, sketch)
    rank_cols = left_factor.shape[1]
    q_blocks = queries.reshape(groups_q, part_rows, head_groups, per_dev * HD)
    q_blocks = q_blocks.transpose(2, 0, 1, 3).reshape(shards, part_rows, per_dev * HD)
    w_blocks = spread_heads(right_factor, head_groups, groups_q, width)
    q_here = lax.all_to_all(q_blocks, "tok", split_axis=0, concat_axis=0, tiled=True)
    u_here = lax.all_gather(left_factor, "tok", axis=0, tiled=True).reshape(
        shards, tok_rows, rank_cols
    )
    w_here = lax.all_to_all(w_blocks, "tok", split_axis=0, concat_axis=0, tiled=True)
    lowrank = jnp.einsum("str,src->stc", u_here, w_here, preferred_element_type=jnp.float32).astype(
        jnp.bfloat16
    )
    lowrank = lowrank.reshape(key_count, per_dev, 2 * HD).transpose(1, 0, 2)
    keys_values = (cache.astype(jnp.float32) + lowrank.astype(jnp.float32)).astype(jnp.bfloat16)
    live_keys = (jnp.arange(tok_rows, dtype=jnp.int32)[None, :] < live_counts[:, None]).reshape(
        key_count
    )
    q_heads = q_here.reshape(query_count, per_dev, HD).transpose(1, 0, 2)
    attended = lax.map(lambda pieces: attend_head(pieces, live_keys), (q_heads, keys_values))
    attended = attended.transpose(1, 0, 2).reshape(shards, part_rows, per_dev * HD)
    returned = lax.all_to_all(attended, "tok", split_axis=0, concat_axis=0, tiled=True)
    returned = returned.reshape(head_groups, groups_q, part_rows, per_dev * HD)
    row_block = returned.transpose(1, 2, 0, 3).reshape(query_rows, head_count * HD)
    return jnp.dot(row_block, w_out, preferred_element_type=jnp.float32).astype(jnp.bfloat16)


def solution(mesh):
    return jax.shard_map(
        per_device,
        mesh=mesh,
        in_specs=(
            P(("groups", "tok"), None),
            P(("groups", "tok"), None),
            P(None, ("groups", "tok"), None),
            P(("groups", "tok")),
            P("groups"),
            P(),
            P(("groups", "tok"), None, None),
            P(),
        ),
        out_specs=P(("groups", "tok"), None),
        check_vma=False,
    )
```

profile of v0, /device:TPU:0, one launch (start us, length us, event | category | flops | bytes accessed | tf_op | source)
XLA Modules:
  0.0 94.7 jit_solution(8483638808945009714)
XLA Ops:
  0.0 1.0 %copy.33 = bf16[4,8,16,128]{3,2,1,0:T(8,128)(2,1)S(1)} copy(bf16[4,8,16,128]{3,1,2,0:T(8,128)(2,1)} %bitcast.116) | data formatting | bytes 262144
  1.0 0.7 copy.43
  1.7 7.4 %all-to-all-start = ((bf16[16,32,128]{2,1,0:T(8,128)(2,1)}), bf16[16,32,128]{2,1,0:T(8,128)(2,1)S(1)}, u32[]{:S(2)}, u32[]{:S(2)}) async-start(bf16[16,32,128]{2,1,0:T(8,128)(2,1)} %bitcast.103), calls=%async_computation | async-start | bytes 262144 | tf_op jit(solution)/shard_map/all_to_all | solution.py:74
  9.7 1.9 %bitcast_subtract_fusion = f32[96,4096]{1,0:T(8,128)S(1)} fusion(bf16[96,4096]{1,0:T(8,128)(2,1)} %param.14, bf16[2,96,4096]{2,1,0:T(8,128)(2,1)} %param.15, pred[]{:T(512)} %bitcast.3), kind=kLoop, calls=%fused_computation.21 | loop fusion | flops 1966080 | bytes 3932161 | tf_op jit(solution)/shard_map/sub | solution.py:68
  11.6 1.3 %fusion.37 = f32[96,32]{0,1:T(8,128)S(1)} fusion(f32[96,4096]{1,0:T(8,128)S(1)} %bitcast_subtract_fusion, f32[4096,32]{0,1:T(8,128)S(1)} %copy-done), kind=kOutput, calls=%fused_computation.61 | convolution fusion | flops 150994944 | bytes 2109440 | tf_op jit(solution)/shard_map/dot_general | solution.py:19
  13.0 0.1 fusion.38
  13.2 2.9 %cholesky.59 = f32[32,32]{1,0:T(8,128)S(1)} custom-call(f32[32,32]{1,0:T(8,128)S(1)} %fusion.31), custom_call_target="Cholesky" | custom-call | tf_op jit(solution)/shard_map/jit(cholesky)/cholesky | solution.py:14
  16.2 0.6 compare_reduce_fusion.2
  16.8 0.7 fusion.17
  17.5 2.4 %custom-call.7 = f32[1,32,32]{1,2,0:T(8,128)S(1)} custom-call(f32[1,32,32]{2,1,0:T(8,128)S(1)} %fusion.17), custom_call_target="InvertDiagBlocksLowerTriangular" | custom-call | tf_op jit(solution)/shard_map/jit(_solve_triangular)/triangular_solve | solution.py:15
  19.9 0.2 fusion.28
  20.1 1.0 %fusion.39 = f32[4096,32]{0,1:T(8,128)S(1)} fusion(f32[96,4096]{1,0:T(8,128)S(1)} %bitcast_subtract_fusion, f32[32,96]{1,0:T(8,128)S(1)} %fusion.28), kind=kOutput, calls=%fused_computation.63 | convolution fusion | flops 150994944 | bytes 2109440 | tf_op jit(solution)/shard_map/dot_general | solution.py:21
  21.2 1.3 %fusion.40 = f32[96,32]{0,1:T(8,128)S(1)} fusion(f32[96,4096]{1,0:T(8,128)S(1)} %bitcast_subtract_fusion, f32[4096,32]{0,1:T(8,128)S(1)} %fusion.39), kind=kOutput, calls=%fused_computation.64 | convolution fusion | flops 150994944 | bytes 2109440 | tf_op jit(solution)/shard_map/dot_general | solution.py:22
  22.5 0.1 fusion.41
  22.7 2.9 %cholesky.70 = f32[32,32]{1,0:T(8,128)S(1)} custom-call(f32[32,32]{1,0:T(8,128)S(1)} %fusion.27), custom_call_target="Cholesky" | custom-call | tf_op jit(solution)/shard_map/jit(cholesky)/cholesky | solution.py:14
  25.7 0.6 compare_reduce_fusion.1
  26.3 0.7 fusion.18
  27.0 2.4 %custom-call.8 = f32[1,32,32]{1,2,0:T(8,128)S(1)} custom-call(f32[1,32,32]{2,1,0:T(8,128)S(1)} %fusion.18), custom_call_target="InvertDiagBlocksLowerTriangular" | custom-call | tf_op jit(solution)/shard_map/jit(_solve_triangular)/triangular_solve | solution.py:15
  29.4 0.2 fusion.24
  29.7 1.0 %fusion.42 = f32[4096,32]{0,1:T(8,128)S(1)} fusion(f32[96,4096]{1,0:T(8,128)S(1)} %bitcast_subtract_fusion, f32[32,96]{1,0:T(8,128)S(1)} %fusion.24), kind=kOutput, calls=%fused_computation.66 | convolution fusion | flops 150994944 | bytes 2109440 | tf_op jit(solution)/shard_map/dot_general | solution.py:21
  30.7 1.3 %fusion.43 = f32[96,32]{0,1:T(8,128)S(1)} fusion(f32[96,4096]{1,0:T(8,128)S(1)} %bitcast_subtract_fusion, f32[4096,32]{0,1:T(8,128)S(1)} %fusion.42), kind=kOutput, calls=%fused_computation.67 | convolution fusion | flops 150994944 | bytes 2109440 | tf_op jit(solution)/shard_map/dot_general | solution.py:22
  32.0 0.1 fusion.44
  32.3 2.9 %cholesky.81 = f32[32,32]{1,0:T(8,128)S(1)} custom-call(f32[32,32]{1,0:T(8,128)S(1)} %fusion.23), custom_call_target="Cholesky" | custom-call | tf_op jit(solution)/shard_map/jit(cholesky)/cholesky | solution.py:14
  35.2 0.6 compare_reduce_fusion
  35.9 0.7 fusion.19
  36.5 2.4 %custom-call.9 = f32[1,32,32]{1,2,0:T(8,128)S(1)} custom-call(f32[1,32,32]{2,1,0:T(8,128)S(1)} %fusion.19), custom_call_target="InvertDiagBlocksLowerTriangular" | custom-call | tf_op jit(solution)/shard_map/jit(_solve_triangular)/triangular_solve | solution.py:15
  39.0 0.2 fusion.20
  39.2 0.9 convolution_convert_fusion
  40.1 0.7 copy.42
  40.8 6.0 %all-to-all-start.1 = ((bf16[16,32,256]{2,1,0:T(8,128)(2,1)}), bf16[16,32,256]{2,1,0:T(8,128)(2,1)S(1)}, u32[]{:S(2)}, u32[]{:S(2)}) async-start(bf16[16,32,256]{2,1,0:T(8,128)(2,1)} %bitcast.102), calls=%async_computation.1 | async-start | bytes 524288 | tf_op jit(solution)/shard_map/all_to_all | solution.py:78
  46.8 22.3 %all-gather = bf16[16,96,32]{1,2,0:T(8,128)(2,1)S(1)} all-gather(bf16[1,96,32]{1,2,0:T(8,128)(2,1)S(1)} %convert_bitcast_fusion), channel_id=1, replica_groups=mesh['groups'=2,'tok'=16] {'tok'}, dimensions={0}, use_global_device_ids=true | all-gather | bytes 104448 | tf_op jit(solution)/shard_map/all_gather | solution.py:75
  69.2 0.1 reshape.49
  69.4 1.6 %fusion.14 = f32[16,96,256]{2,1,0:T(8,128)} fusion(bf16[16,96,32]{1,2,0:T(8,128)(2,1)S(1)} %all-gather, bf16[16,32,256]{2,1,0:T(8,128)(2,1)S(1)} %all-to-all-done.1), kind=kOutput, calls=%fused_computation.23 | convolution fusion | flops 25952256 | bytes 1933312 | tf_op jit(solution)/shard_map/str,src->stc/dot_general | solution.py:79
  71.0 2.1 %reshape.55 = f32[1536,2,128]{2,1,0:T(2,128)S(1)} reshape(f32[16,96,256]{2,1,0:T(8,128)} %fusion.14) | data formatting | bytes 3145728 | tf_op jit(solution)/shard_map/convert_element_type | solution.py:83
  73.0 1.3 %fusion.13 = bf16[2,1536,128]{2,1,0:T(8,128)(2,1)S(1)} fusion(f32[1536,2,128]{2,1,0:T(2,128)S(1)} %reshape.55, bf16[2,1536,128]{2,1,0:T(8,128)(2,1)} %param.19), kind=kLoop, calls=%fused_computation.20 | loop fusion | flops 1179648 | bytes 3145728 | tf_op jit(solution)/shard_map/convert_element_type | solution.py:83
  74.3 4.9 %while.11 = (s32[]{:T(128)}, bf16[2,512,64]{1,2,0:T(8,128)(2,1)S(1)}, bf16[2,512,64]{2,1,0:T(8,128)(2,1)S(1)}, bf16[2,1536,128]{2,1,0:T(8,128)(2,1)S(1)}, s32[16]{0:T(128)S(1)}, /*index=5*/s32[]{:T(128)}) while((s32[]{:T(128)}, bf16[2,512,64]{1,2,0:T(8,128)(2,1)S(1)}, bf16[2,512,64]{2,1,0:T(8,128)(2,1)S(1)}, ...), condition=%wide.region_5.8_spmd.clone, body=%wide.region_2.7_spmd.clone.sunk | while | flops 207651328 | bytes 11223697 | solution.py:88
  74.5 0.1 broadcast_in_dim.43
  74.5 0.7 fusion.71
  75.2 0.6 fusion.72
  75.8 1.0 %fusion.73 = bf16[2,512,64]{1,2,0:T(8,128)(2,1)S(1)} fusion(bf16[2,512,64]{1,2,0:T(8,128)(2,1)S(1)} %get-tuple-element.130, s32[]{:T(128)} %get-tuple-element.129, f32[512,1536]{1,0:T(8,128)S(1)} %get-tuple-element.121, f32[512]{0:T(512)S(1)} %fusion.72, f32[512]{0:T(512)S(1)} %get-tuple-element.122, ...), kind=kOutput, calls=%fused_computation.9.clone.1 | convolution fusion | flops 103055360 | bytes 3608580 | tf_op jit(solution)/shard_map/while/body/eval_jaxpr/while/body/eval_jaxpr/dot_general | solution.py:47
  76.9 0.1 broadcast_in_dim.43
  77.0 0.7 fusion.71
  77.7 0.6 fusion.72
  78.3 1.0 %fusion.73 = bf16[2,512,64]{1,2,0:T(8,128)(2,1)S(1)} fusion(bf16[2,512,64]{1,2,0:T(8,128)(2,1)S(1)} %get-tuple-element.130, s32[]{:T(128)} %get-tuple-element.129, f32[512,1536]{1,0:T(8,128)S(1)} %get-tuple-element.121, f32[512]{0:T(512)S(1)} %fusion.72, f32[512]{0:T(512)S(1)} %get-tuple-element.122, ...), kind=kOutput, calls=%fused_computation.9.clone.1 | convolution fusion | flops 103055360 | bytes 3608580 | tf_op jit(solution)/shard_map/while/body/eval_jaxpr/while/body/eval_jaxpr/dot_general | solution.py:47
  79.3 0.2 copy.30
  79.4 0.1 reshape.52
  79.6 10.5 %all_to_all.15 = bf16[16,32,128]{2,1,0:T(8,128)(2,1)S(1)} all-to-all(bf16[16,32,128]{2,1,0:T(8,128)(2,1)S(1)} %reshape.52), channel_id=1, replica_groups=mesh['groups'=2,'tok'=16] {'tok'}, dimensions={0} | all-to-all | bytes 262144 | tf_op jit(solution)/shard_map/all_to_all | solution.py:90
  90.1 4.6 %convolution_convert_fusion.1 = bf16[32,1536]{1,0:T(8,128)(2,1)} fusion(bf16[2048,1536]{1,0:T(8,128)(2,1)} %param.20, bf16[4,8,16,128]{3,2,1,0:T(8,128)(2,1)S(1)} %bitcast.112), kind=kOutput, calls=%fused_computation.18 | convolution fusion | flops 201375744 | bytes 6520832 | tf_op jit(solution)/shard_map/dot_general | solution.py:93
  (23 shorter events, 0.7 us)
Async XLA Ops:
  0.0 11.6 %copy-start = (f32[4096,32]{0,1:T(8,128)S(1)}, f32[4096,32]{0,1:T(8,128)}, u32[]{:S(2)}) copy-start(f32[4096,32]{0,1:T(8,128)} %param.18) | copy-start | bytes 1572868
  1.7 39.1 %all-to-all-start = ((bf16[16,32,128]{2,1,0:T(8,128)(2,1)}), bf16[16,32,128]{2,1,0:T(8,128)(2,1)S(1)}, u32[]{:S(2)}, u32[]{:S(2)}) async-start(bf16[16,32,128]{2,1,0:T(8,128)(2,1)} %bitcast.103), calls=%async_computation | async-start | bytes 262144 | tf_op jit(solution)/shard_map/all_to_all | solution.py:74
  40.8 28.6 %all-to-all-start.1 = ((bf16[16,32,256]{2,1,0:T(8,128)(2,1)}), bf16[16,32,256]{2,1,0:T(8,128)(2,1)S(1)}, u32[]{:S(2)}, u32[]{:S(2)}) async-start(bf16[16,32,256]{2,1,0:T(8,128)(2,1)} %bitcast.102), calls=%async_computation.1 | async-start | bytes 524288 | tf_op jit(solution)/shard_map/all_to_all | solution.py:78
  73.0 1.3 %copy-start.1 = (s32[16]{0:T(128)S(1)}, s32[16]{0:T(128)}, u32[]{:S(2)}) copy-start(s32[16]{0:T(128)} %param.17) | copy-start | bytes 196
where the time goes:
time: 95.2 us; the launch traced here: 94.7 us
  blocking collectives  32.8 us (34%)
  other arithmetic  24.6 us (26%)
  matrix products  17.5 us (18%)
  starting transfers between devices  13.4 us (14%)
  local copies, waits for them, and re-layouts  5.45 us (6%)
    all_gather x1, blocking collectives, per_device(): lax.all_gather(left_factor, 'tok', axis=0, tiled=True)  22.3 us
    another operation x9, other arithmetic, orthonormal(): lower_factor = jnp.linalg.cholesky(gram_matrix)  10.8 us
    all_to_all x1, blocking collectives, per_device(): lax.all_to_all(attended, 'tok', split_axis=0, concat_axis=0, tiled=True)  10.5 us
    another operation x6, other arithmetic, orthonormal(): jax.scipy.linalg.solve_triangular(lower_factor, block_cols.T, lower=True)  9.26 us
    all_to_all x1, starting transfers between devices, per_device(): lax.all_to_all(q_blocks, 'tok', split_axis=0, concat_axis=0, tiled=True)  7.39 us
    all_to_all x1, starting transfers between devices, per_device(): lax.all_to_all(w_blocks, 'tok', split_axis=0, concat_axis=0, tiled=True)  6.01 us
    dot_general x1, matrix products, per_device(): jnp.dot(row_block, w_out, preferred_element_type=jnp.float32)  4.56 us
    dot_general x2, matrix products, compress(): basis_cols = orthonormal(jnp.dot(delta_block, inner, precision=highest))  2.69 us
  transfers between devices with their start and end apart: 2, of which 0 were waited for; matrix products, arithmetic and copies ran while one was open for 33% of the time, Pallas kernels for 0%

commit v1 on v0

--- a/solution.py
+++ b/solution.py
@@ -72,9 +72,9 @@
     q_blocks = q_blocks.transpose(2, 0, 1, 3).reshape(shards, part_rows, per_dev * HD)
     w_blocks = spread_heads(right_factor, head_groups, groups_q, width)
     q_here = lax.all_to_all(q_blocks, "tok", split_axis=0, concat_axis=0, tiled=True)
-    u_here = lax.all_gather(left_factor, "tok", axis=0, tiled=True).reshape(
-        shards, tok_rows, rank_cols
-    )
+    u_here = jnp.concatenate(
+        lax.all_to_all(jnp.stack([left_factor] * lax.axis_size("tok")), "tok", 0, 0), axis=0
+    ).reshape(shards, tok_rows, rank_cols)
     w_here = lax.all_to_all(w_blocks, "tok", split_axis=0, concat_axis=0, tiled=True)
     lowrank = jnp.einsum("str,src->stc", u_here, w_here, preferred_element_type=jnp.float32).astype(
         jnp.bfloat16

time: 95.2 us -> 97.1 us (1.020)
  waiting for transfers between devices: 0.01 us -> 23.1 us
  blocking collectives: 32.8 us -> 10.7 us
  starting transfers between devices: 13.4 us -> 14.6 us
    all_gather x1 -> x0, blocking collectives: 22.3 us -> none  [per_device(): lax.all_gather(left_factor, 'tok', axis=0, tiled=True)]
    all_to_all x1, waiting for transfers between devices: 0.01 us -> 9.6 us  [per_device(): lax.all_to_all(w_blocks, 'tok', split_axis=0, concat_axis=0, tiled=True)]
    all_to_all x0 -> x1, starting transfers between devices: none -> 7.39 us  [per_device(): lax.all_to_all(jnp.stack([left_factor] * lax.axis_size('tok')), 'tok', 0, 0)]
    all_to_all x0 -> x1, waiting for transfers between devices: none -> 7.17 us  [per_device(): lax.all_to_all(jnp.stack([left_factor] * lax.axis_size('tok')), 'tok', 0, 0)]
    all_to_all x1, waiting for transfers between devices: 0.01 us -> 6.28 us  [per_device(): lax.all_to_all(q_blocks, 'tok', split_axis=0, concat_axis=0, tiled=True)]
    all_to_all x1, starting transfers between devices: 7.39 us -> 3.51 us  [per_device(): lax.all_to_all(q_blocks, 'tok', split_axis=0, concat_axis=0, tiled=True)]
    all_to_all x1, starting transfers between devices: 6.01 us -> 3.71 us  [per_device(): lax.all_to_all(w_blocks, 'tok', split_axis=0, concat_axis=0, tiled=True)]
  transfers between devices with their start and end apart: 2 -> 3, of which waited for: 0 -> 3; matrix products, arithmetic and copies ran while one was open for 33% -> 3% of each run, Pallas kernels for 0% -> 0%
where the time goes in v1:
time: 97.1 us; the launch traced here: 96.6 us
  other arithmetic  24.6 us (25%)
  waiting for transfers between devices  23.1 us (24%)
  matrix products  17.5 us (18%)
  starting transfers between devices  14.6 us (15%)
  blocking collectives  10.7 us (11%)
  local copies, waits for them, and re-layouts  5.15 us (5%)
  between operations  1.01 us (1%)
    another operation x9, other arithmetic, orthonormal(): lower_factor = jnp.linalg.cholesky(gram_matrix)  10.8 us
    all_to_all x1, blocking collectives, per_device(): lax.all_to_all(attended, 'tok', split_axis=0, concat_axis=0, tiled=True)  10.7 us
    all_to_all x1, waiting for transfers between devices, per_device(): lax.all_to_all(w_blocks, 'tok', split_axis=0, concat_axis=0, tiled=True)  9.6 us
    another operation x6, other arithmetic, orthonormal(): jax.scipy.linalg.solve_triangular(lower_factor, block_cols.T, lower=True)  9.26 us
    all_to_all x1, starting transfers between devices, per_device(): lax.all_to_all(jnp.stack([left_factor] * lax.axis_size('tok')), 'tok', 0, 0)  7.39 us
    all_to_all x1, waiting for transfers between devices, per_device(): lax.all_to_all(jnp.stack([left_factor] * lax.axis_size('tok')), 'tok', 0, 0)  7.17 us
    all_to_all x1, waiting for transfers between devices, per_device(): lax.all_to_all(q_blocks, 'tok', split_axis=0, concat_axis=0, tiled=True)  6.28 us
    dot_general x1, matrix products, per_device(): jnp.dot(row_block, w_out, preferred_element_type=jnp.float32)  4.56 us
  transfers between devices with their start and end apart: 3, of which 3 were waited for; matrix products, arithmetic and copies ran while one was open for 3% of the time, Pallas kernels for 0%

profile of v1, /device:TPU:0, one launch (start us, length us, event | category | flops | bytes accessed | tf_op | source)
XLA Modules:
  0.0 96.6 jit_solution(9562710304180005357)
XLA Ops:
  0.7 1.9 %bitcast_subtract_fusion = f32[96,4096]{1,0:T(8,128)S(1)} fusion(bf16[96,4096]{1,0:T(8,128)(2,1)} %param.14, bf16[2,96,4096]{2,1,0:T(8,128)(2,1)} %param.15, pred[]{:T(512)} %bitcast.3), kind=kLoop, calls=%fused_computation.21 | loop fusion | flops 1966080 | bytes 3932161 | tf_op jit(solution)/shard_map/sub | solution.py:68
  2.6 1.3 %fusion.37 = f32[96,32]{0,1:T(8,128)S(1)} fusion(f32[96,4096]{1,0:T(8,128)S(1)} %bitcast_subtract_fusion, f32[4096,32]{0,1:T(8,128)S(1)} %copy-done), kind=kOutput, calls=%fused_computation.61 | convolution fusion | flops 150994944 | bytes 2109440 | tf_op jit(solution)/shard_map/dot_general | solution.py:19
  4.0 0.1 fusion.38
  4.2 2.9 %cholesky.59 = f32[32,32]{1,0:T(8,128)S(1)} custom-call(f32[32,32]{1,0:T(8,128)S(1)} %fusion.31), custom_call_target="Cholesky" | custom-call | tf_op jit(solution)/shard_map/jit(cholesky)/cholesky | solution.py:14
  7.2 0.6 compare_reduce_fusion.2
  7.8 0.7 fusion.17
  8.5 2.4 %custom-call.7 = f32[1,32,32]{1,2,0:T(8,128)S(1)} custom-call(f32[1,32,32]{2,1,0:T(8,128)S(1)} %fusion.17), custom_call_target="InvertDiagBlocksLowerTriangular" | custom-call | tf_op jit(solution)/shard_map/jit(_solve_triangular)/triangular_solve | solution.py:15
  10.9 0.2 fusion.28
  11.1 1.0 %fusion.39 = f32[4096,32]{0,1:T(8,128)S(1)} fusion(f32[96,4096]{1,0:T(8,128)S(1)} %bitcast_subtract_fusion, f32[32,96]{1,0:T(8,128)S(1)} %fusion.28), kind=kOutput, calls=%fused_computation.63 | convolution fusion | flops 150994944 | bytes 2109440 | tf_op jit(solution)/shard_map/dot_general | solution.py:21
  12.1 1.3 %fusion.40 = f32[96,32]{0,1:T(8,128)S(1)} fusion(f32[96,4096]{1,0:T(8,128)S(1)} %bitcast_subtract_fusion, f32[4096,32]{0,1:T(8,128)S(1)} %fusion.39), kind=kOutput, calls=%fused_computation.64 | convolution fusion | flops 150994944 | bytes 2109440 | tf_op jit(solution)/shard_map/dot_general | solution.py:22
  13.5 0.1 fusion.41
  13.7 2.9 %cholesky.70 = f32[32,32]{1,0:T(8,128)S(1)} custom-call(f32[32,32]{1,0:T(8,128)S(1)} %fusion.27), custom_call_target="Cholesky" | custom-call | tf_op jit(solution)/shard_map/jit(cholesky)/cholesky | solution.py:14
  16.7 0.6 compare_reduce_fusion.1
  17.3 0.7 fusion.18
  18.0 2.4 %custom-call.8 = f32[1,32,32]{1,2,0:T(8,128)S(1)} custom-call(f32[1,32,32]{2,1,0:T(8,128)S(1)} %fusion.18), custom_call_target="InvertDiagBlocksLowerTriangular" | custom-call | tf_op jit(solution)/shard_map/jit(_solve_triangular)/triangular_solve | solution.py:15
  20.4 0.2 fusion.24
  20.7 1.0 %fusion.42 = f32[4096,32]{0,1:T(8,128)S(1)} fusion(f32[96,4096]{1,0:T(8,128)S(1)} %bitcast_subtract_fusion, f32[32,96]{1,0:T(8,128)S(1)} %fusion.24), kind=kOutput, calls=%fused_computation.66 | convolution fusion | flops 150994944 | bytes 2109440 | tf_op jit(solution)/shard_map/dot_general | solution.py:21
  21.7 1.3 %fusion.43 = f32[96,32]{0,1:T(8,128)S(1)} fusion(f32[96,4096]{1,0:T(8,128)S(1)} %bitcast_subtract_fusion, f32[4096,32]{0,1:T(8,128)S(1)} %fusion.42), kind=kOutput, calls=%fused_computation.67 | convolution fusion | flops 150994944 | bytes 2109440 | tf_op jit(solution)/shard_map/dot_general | solution.py:22
  23.0 0.1 fusion.44
  23.3 2.9 %cholesky.81 = f32[32,32]{1,0:T(8,128)S(1)} custom-call(f32[32,32]{1,0:T(8,128)S(1)} %fusion.23), custom_call_target="Cholesky" | custom-call | tf_op jit(solution)/shard_map/jit(cholesky)/cholesky | solution.py:14
  26.2 0.6 compare_reduce_fusion
  26.9 0.7 fusion.19
  27.5 2.4 %custom-call.9 = f32[1,32,32]{1,2,0:T(8,128)S(1)} custom-call(f32[1,32,32]{2,1,0:T(8,128)S(1)} %fusion.19), custom_call_target="InvertDiagBlocksLowerTriangular" | custom-call | tf_op jit(solution)/shard_map/jit(_solve_triangular)/triangular_solve | solution.py:15
  30.0 0.2 fusion.20
  30.2 0.7 stack.2
  30.9 7.4 %all-to-all-start.1 = ((bf16[16,96,32]{1,2,0:T(8,128)(2,1)}), bf16[16,96,32]{1,2,0:T(8,128)(2,1)S(1)}, u32[]{:S(2)}, u32[]{:S(2)}) async-start(bf16[16,96,32]{1,2,0:T(8,128)(2,1)} %stack.2), calls=%async_computation.1 | async-start | bytes 262144 | tf_op jit(solution)/shard_map/all_to_all | solution.py:76
  38.3 0.7 copy.43
  39.0 7.2 %all-to-all-done.1 = bf16[16,96,32]{1,2,0:T(8,128)(2,1)S(1)} async-done(((bf16[16,96,32]{1,2,0:T(8,128)(2,1)}), bf16[16,96,32]{1,2,0:T(8,128)(2,1)S(1)}, u32[]{:S(2)}, u32[]{:S(2)}) %all-to-all-start.1) | async-done | bytes 98336 | tf_op jit(solution)/shard_map/all_to_all | solution.py:76
  46.2 3.5 %all-to-all-start = ((bf16[16,32,128]{2,1,0:T(8,128)(2,1)}), bf16[16,32,128]{2,1,0:T(8,128)(2,1)S(1)}, u32[]{:S(2)}, u32[]{:S(2)}) async-start(bf16[16,32,128]{2,1,0:T(8,128)(2,1)} %bitcast.101), calls=%async_computation | async-start | bytes 262144 | tf_op jit(solution)/shard_map/all_to_all | solution.py:74
  49.7 0.9 convolution_convert_fusion
  50.6 0.7 copy.42
  51.3 6.3 %all-to-all-done = bf16[16,32,128]{2,1,0:T(8,128)(2,1)S(1)} async-done(((bf16[16,32,128]{2,1,0:T(8,128)(2,1)}), bf16[16,32,128]{2,1,0:T(8,128)(2,1)S(1)}, u32[]{:S(2)}, u32[]{:S(2)}) %all-to-all-start) | async-done | bytes 131104 | tf_op jit(solution)/shard_map/all_to_all | solution.py:74
  57.6 3.7 %all-to-all-start.2 = ((bf16[16,32,256]{2,1,0:T(8,128)(2,1)}), bf16[16,32,256]{2,1,0:T(8,128)(2,1)S(1)}, u32[]{:S(2)}, u32[]{:S(2)}) async-start(bf16[16,32,256]{2,1,0:T(8,128)(2,1)} %bitcast.100), calls=%async_computation.2 | async-start | bytes 524288 | tf_op jit(solution)/shard_map/all_to_all | solution.py:78
  61.5 9.6 %all-to-all-done.2 = bf16[16,32,256]{2,1,0:T(8,128)(2,1)S(1)} async-done(((bf16[16,32,256]{2,1,0:T(8,128)(2,1)}), bf16[16,32,256]{2,1,0:T(8,128)(2,1)S(1)}, u32[]{:S(2)}, u32[]{:S(2)}) %all-to-all-start.2) | async-done | bytes 262176 | tf_op jit(solution)/shard_map/all_to_all | solution.py:78
  71.1 1.6 %fusion.14 = f32[16,96,256]{2,1,0:T(8,128)} fusion(bf16[16,96,32]{1,2,0:T(8,128)(2,1)S(1)} %all-to-all-done.1, bf16[16,32,256]{2,1,0:T(8,128)(2,1)S(1)} %all-to-all-done.2), kind=kOutput, calls=%fused_computation.23 | convolution fusion | flops 25952256 | bytes 1933312 | tf_op jit(solution)/shard_map/str,src->stc/dot_general | solution.py:79
  72.7 2.1 %reshape.53 = f32[1536,2,128]{2,1,0:T(2,128)S(1)} reshape(f32[16,96,256]{2,1,0:T(8,128)} %fusion.14) | data formatting | bytes 3145728 | tf_op jit(solution)/shard_map/convert_element_type | solution.py:83
  74.7 1.3 %fusion.13 = bf16[2,1536,128]{2,1,0:T(8,128)(2,1)S(1)} fusion(f32[1536,2,128]{2,1,0:T(2,128)S(1)} %reshape.53, bf16[2,1536,128]{2,1,0:T(8,128)(2,1)} %param.19), kind=kLoop, calls=%fused_computation.20 | loop fusion | flops 1179648 | bytes 3145728 | tf_op jit(solution)/shard_map/convert_element_type | solution.py:83
  76.0 4.9 %while.11 = (s32[]{:T(128)}, bf16[2,512,64]{1,2,0:T(8,128)(2,1)S(1)}, bf16[2,512,64]{2,1,0:T(8,128)(2,1)S(1)}, bf16[2,1536,128]{2,1,0:T(8,128)(2,1)S(1)}, s32[16]{0:T(128)S(1)}, /*index=5*/s32[]{:T(128)}) while((s32[]{:T(128)}, bf16[2,512,64]{1,2,0:T(8,128)(2,1)S(1)}, bf16[2,512,64]{2,1,0:T(8,128)(2,1)S(1)}, ...), condition=%wide.region_5.8_spmd.clone, body=%wide.region_2.7_spmd.clone.sunk | while | flops 207651328 | bytes 11223697 | solution.py:88
  76.2 0.7 fusion.71
  76.9 0.6 fusion.72
  77.5 1.0 %fusion.73 = bf16[2,512,64]{1,2,0:T(8,128)(2,1)S(1)} fusion(bf16[2,512,64]{1,2,0:T(8,128)(2,1)S(1)} %get-tuple-element.130, s32[]{:T(128)} %get-tuple-element.129, f32[512,1536]{1,0:T(8,128)S(1)} %get-tuple-element.121, f32[512]{0:T(512)S(1)} %fusion.72, f32[512]{0:T(512)S(1)} %get-tuple-element.122, ...), kind=kOutput, calls=%fused_computation.9.clone.1 | convolution fusion | flops 103055360 | bytes 3608580 | tf_op jit(solution)/shard_map/while/body/eval_jaxpr/while/body/eval_jaxpr/dot_general | solution.py:47
  78.7 0.7 fusion.71
  79.4 0.6 fusion.72
  80.0 1.0 %fusion.73 = bf16[2,512,64]{1,2,0:T(8,128)(2,1)S(1)} fusion(bf16[2,512,64]{1,2,0:T(8,128)(2,1)S(1)} %get-tuple-element.130, s32[]{:T(128)} %get-tuple-element.129, f32[512,1536]{1,0:T(8,128)S(1)} %get-tuple-element.121, f32[512]{0:T(512)S(1)} %fusion.72, f32[512]{0:T(512)S(1)} %get-tuple-element.122, ...), kind=kOutput, calls=%fused_computation.9.clone.1 | convolution fusion | flops 103055360 | bytes 3608580 | tf_op jit(solution)/shard_map/while/body/eval_jaxpr/while/body/eval_jaxpr/dot_general | solution.py:47
  81.0 0.2 copy.30
  81.1 0.1 reshape.50
  81.3 10.7 %all_to_all.20 = bf16[16,32,128]{2,1,0:T(8,128)(2,1)S(1)} all-to-all(bf16[16,32,128]{2,1,0:T(8,128)(2,1)S(1)} %reshape.50), channel_id=1, replica_groups=mesh['groups'=2,'tok'=16] {'tok'}, dimensions={0} | all-to-all | bytes 262144 | tf_op jit(solution)/shard_map/all_to_all | solution.py:90
  92.0 4.6 %convolution_convert_fusion.1 = bf16[32,1536]{1,0:T(8,128)(2,1)} fusion(bf16[2048,1536]{1,0:T(8,128)(2,1)} %param.20, bf16[4,8,16,128]{3,2,1,0:T(8,128)(2,1)S(1)} %bitcast.110), kind=kOutput, calls=%fused_computation.18 | convolution fusion | flops 201375744 | bytes 6520832 | tf_op jit(solution)/shard_map/dot_general | solution.py:93
  (27 shorter events, 1.0 us)
Async XLA Ops:
  0.0 2.6 %copy-start = (f32[4096,32]{0,1:T(8,128)S(1)}, f32[4096,32]{0,1:T(8,128)}, u32[]{:S(2)}) copy-start(f32[4096,32]{0,1:T(8,128)} %param.18) | copy-start | bytes 1572868
  21.7 16.6 %copy-start.1 = (bf16[32,2048]{1,0:T(8,128)(2,1)S(1)}, bf16[32,2048]{1,0:T(8,128)(2,1)}, u32[]{:S(2)}) copy-start(bf16[32,2048]{1,0:T(8,128)(2,1)} %param.13) | copy-start | bytes 393220
  30.9 15.3 %all-to-all-start.1 = ((bf16[16,96,32]{1,2,0:T(8,128)(2,1)}), bf16[16,96,32]{1,2,0:T(8,128)(2,1)S(1)}, u32[]{:S(2)}, u32[]{:S(2)}) async-start(bf16[16,96,32]{1,2,0:T(8,128)(2,1)} %stack.2), calls=%async_computation.1 | async-start | bytes 262144 | tf_op jit(solution)/shard_map/all_to_all | solution.py:76
  46.2 11.4 %all-to-all-start = ((bf16[16,32,128]{2,1,0:T(8,128)(2,1)}), bf16[16,32,128]{2,1,0:T(8,128)(2,1)S(1)}, u32[]{:S(2)}, u32[]{:S(2)}) async-start(bf16[16,32,128]{2,1,0:T(8,128)(2,1)} %bitcast.101), calls=%async_computation | async-start | bytes 262144 | tf_op jit(solution)/shard_map/all_to_all | solution.py:74
  57.6 13.5 %all-to-all-start.2 = ((bf16[16,32,256]{2,1,0:T(8,128)(2,1)}), bf16[16,32,256]{2,1,0:T(8,128)(2,1)S(1)}, u32[]{:S(2)}, u32[]{:S(2)}) async-start(bf16[16,32,256]{2,1,0:T(8,128)(2,1)} %bitcast.100), calls=%async_computation.2 | async-start | bytes 524288 | tf_op jit(solution)/shard_map/all_to_all | solution.py:78
  74.7 1.3 %copy-start.2 = (s32[16]{0:T(128)S(1)}, s32[16]{0:T(128)}, u32[]{:S(2)}) copy-start(s32[16]{0:T(128)} %param.17) | copy-start | bytes 196
